TPU v7x, 32 devices: a whole 2x2x4 slice. The times are simulated.
32 devices in a mesh: blk: 8 (over y, x, core), feat: 4 (over z).
Axes of the slice: x: 2, y: 2, z: 4, core: 2. Of those that a mesh axis runs over, the one named last changes fastest.
Arguments:
- node_feats: bfloat16 [8192, 512], P('blk', 'feat'), may hold values from -6 to 6
- weight: bfloat16 [512, 512], P(None, 'feat'), may hold values from -0.25 to 0.25
- tile_value: bfloat16 [8, 5, 8, 128, 128], P('blk'), may hold values from -0.75 to 0.75
- tile_row: int32 [8, 5, 8], P('blk'), may hold values from 0 to 7
- tile_col: int32 [8, 5, 8], P('blk'), may hold values from 0 to 7
- tile_count: int32 [8, 5], P('blk'), may hold values from 2 to 8, as said below
- grad_out: bfloat16 [8192, 512], P('blk', 'feat'), may hold values from -6 to 6
Outputs:
- output_y: bfloat16 [8192, 512], P('blk', 'feat')
- grad_x: bfloat16 [8192, 512], P('blk', 'feat')
- grad_w: float32 [512, 512], P(None, 'feat')
Inputs may be any that keep to these rules, and one draw needn't show every extreme that they name: `tile_count`: in every draw one owner has all 8 slots live for every distance; owners differ in how many tiles they hold.
All inputs are finite; a program needn't handle non-finite values.
Results may differ from a plain program's by a relative error of at most 0.0062.
Values may be sent and summed in bfloat16 or wider, within the bound.
A program may use at most 64 MiB of HBM per device.

v0:
```python
import jax
import jax.numpy as jnp
from jax import lax
from jax.sharding import PartitionSpec as P


def shifted(block, axis, distance):
    devices = range(lax.axis_size(axis))
    route = [((i - distance) % len(devices), i) for i in devices]
    return lax.ppermute(block, axis, route)


def on_device(node_feats, weight, tile_value, tile_row, tile_col, tile_count, grad_out):
    tile_side = tile_value.shape[-1]
    blocks = node_feats.shape[0] // tile_side
    feat_width = weight.shape[1]
    offsets = tile_value.shape[1]
    reach_count = (offsets - 1) // 2
    slot_ids = jnp.arange(tile_value.shape[2], dtype=jnp.int32)
    block_ids = jnp.arange(blocks, dtype=jnp.int32)
    live_slots = slot_ids[None, :] < tile_count[0][:, None]
    row_onehot = (
        (tile_row[0][:, None, :] == block_ids[None, :, None]) & live_slots[:, None, :]
    ).astype(jnp.float32)
    col_onehot = (
        (tile_col[0][:, None, :] == block_ids[None, :, None]) & live_slots[:, None, :]
    ).astype(jnp.float32)
    full_feats = lax.all_gather(node_feats, "feat", axis=1, tiled=True)
    hidden = jnp.dot(full_feats, weight, preferred_element_type=jnp.float32).astype(jnp.bfloat16)
    panel_own = hidden.reshape(blocks, tile_side, feat_width)
    wanted_lists = {}
    picked = jnp.take(panel_own, tile_col[0, reach_count], axis=0)
    gather_product = jnp.einsum(
        "sij,sjf->sif", tile_value[0, reach_count], picked, preferred_element_type=jnp.float32
    )
    aggregate = jnp.einsum(
        "rs,sif->rif", row_onehot[reach_count], gather_product, precision=lax.Precision.HIGHEST
    )
    for distance in range(-reach_count, reach_count + 1):
        if distance != 0:
            offset = distance + reach_count
            wanted = shifted(tile_col[0, offset], "blk", distance)
            wanted_lists[distance] = wanted
            sent_blocks = jnp.take(panel_own, wanted, axis=0)
            arrived = shifted(sent_blocks, "blk", -distance)
            product = jnp.einsum(
                "sij,sjf->sif", tile_value[0, offset], arrived, preferred_element_type=jnp.float32
            )
            aggregate = aggregate + jnp.einsum(
                "rs,sif->rif", row_onehot[offset], product, precision=lax.Precision.HIGHEST
            )
    preact = aggregate.reshape(blocks * tile_side, feat_width) + hidden.astype(jnp.float32)
    output_y = jax.nn.silu(preact).astype(jnp.bfloat16)
    sigmoid_pre = jax.nn.sigmoid(preact)
    slope_term = sigmoid_pre * (1.0 + preact * (1.0 - sigmoid_pre))
    grad_pre = (grad_out.astype(jnp.float32) * slope_term).astype(jnp.bfloat16)
    grad_blocks = grad_pre.reshape(blocks, tile_side, feat_width)

    def slot_products(offset):
        picked = jnp.take(grad_blocks, tile_row[0, offset], axis=0)
        return jnp.einsum(
            "sji,sjf->sif", tile_value[0, offset], picked, preferred_element_type=jnp.float32
        )

    transposed = jnp.einsum(
        "cs,sif->cif",
        col_onehot[reach_count],
        slot_products(reach_count),
        precision=lax.Precision.HIGHEST,
    )
    for distance in range(-reach_count, reach_count + 1):
        if distance != 0:
            offset = distance + reach_count
            masked = slot_products(offset) * live_slots[offset][:, None, None].astype(jnp.float32)
            received = shifted(masked, "blk", distance)
            target_onehot = (wanted_lists[distance][None, :] == block_ids[:, None]).astype(
                jnp.float32
            )
            transposed = transposed + jnp.einsum(
                "cs,sif->cif", target_onehot, received, precision=lax.Precision.HIGHEST
            )
    grad_hidden = (
        grad_pre.astype(jnp.float32) + transposed.reshape(blocks * tile_side, feat_width)
    ).astype(jnp.bfloat16)
    weight_term = lax.dot_general(
        full_feats, grad_hidden, (((0,), (0,)), ((), ())), preferred_element_type=jnp.float32
    )
    grad_w = lax.psum(weight_term, "blk")
    partial_grad = lax.dot_general(
        grad_hidden, weight, (((1,), (1,)), ((), ())), preferred_element_type=jnp.float32
    )
    grad_x = lax.psum_scatter(partial_grad, "feat", scatter_dimension=1, tiled=True).astype(
        jnp.bfloat16
    )
    return (output_y, grad_x, grad_w)


def solution(mesh):
    return jax.shard_map(
        on_device,
        mesh=mesh,
        in_specs=(
            P("blk", "feat"),
            P(None, "feat"),
            P("blk", None, None, None, None),
            P("blk", None, None),
            P("blk", None, None),
            P("blk", None),
            P("blk", "feat"),
        ),
        out_specs=(P("blk", "feat"), P("blk", "feat"), P(None, "feat")),
        check_vma=False,
    )
```

profile of v0, /device:TPU:0, one launch (start us, length us, event | category | flops | bytes accessed | tf_op | source)
XLA Modules:
  0.0 216.4 jit_solution(13034620834880448403)
XLA Ops:
  7.2 0.7 all-gather.2.cloned.1.call-update
  8.0 0.7 slice_bitcast_fusion.10
  8.7 3.9 %collective-permute-start = (s32[8]{0:T(128)S(1)}, s32[8]{0:T(128)S(1)}, u32[]{:S(2)}, u32[]{:S(2)}) collective-permute-start(s32[8]{0:T(128)S(1)} %get-tuple-element.32), channel_id=1, source_target_pairs={{8,0},{12,4},{16,8},{20,12},{24,16},{28,20},{0,24},{4,28},{9,1},{1... | collective-permute-start | bytes 104 | tf_op jit(solution)/shard_map/ppermute | solution.py:10
  13.1 0.7 collective-permute-start.6
  13.8 0.7 compare_and_fusion.9
  14.4 0.7 copy.28
  15.1 1.3 compare_and_fusion.2
  16.4 0.7 copy.27
  17.1 0.7 iota_compare_fusion.6
  17.9 0.6 fusion.80
  18.5 0.5 slice.130
  19.0 0.6 pad_clamp_fusion.2
  19.6 0.6 pad_clamp_fusion
  20.3 0.6 pad_clamp_fusion.6
  21.0 0.5 compare_and_fusion.7
  21.5 0.5 compare_and_fusion.6
  22.0 0.6 compare_and_fusion.5
  22.6 19.6 %all-gather.2.cloned.1.call-done = bf16[1024,512]{1,0:T(8,128)(2,1)} async-done(((bf16[1024,128]{1,0:T(8,128)(2,1)}), bf16[1024,512]{1,0:T(8,128)(2,1)}) %all-gather.2.cloned.1.call-update) | async-done | bytes 1048592 | tf_op jit(solution)/shard_map/all_gather | solution.py:28
  42.2 1.7 convolution_convert_fusion
  43.9 0.6 gather_fusion.1
  44.6 0.7 collective-permute-start.1
  45.3 0.6 gather_fusion
  46.7 0.6 gather_fusion.2
  47.3 0.7 broadcast_select_fusion.2
  48.1 0.7 gather_fusion.3
  48.9 0.8 broadcast_select_fusion.1
  49.6 2.6 %collective-permute-start.5 = (bf16[8,128,128]{2,1,0:T(8,128)(2,1)}, bf16[8,128,128]{2,1,0:T(8,128)(2,1)}, u32[]{:S(2)}, u32[]{:S(2)}) collective-permute-start(bf16[8,128,128]{2,1,0:T(8,128)(2,1)} %broadcast_select_fusion.1), channel_id=1, source_target_pairs={{4,0},{8,4},{12,8},{16,12},{20,16},{24,20},{28,24},{0,28},{5,1},{9... | collective-permute-start | bytes 786440 | tf_op jit(solution)/shard_map/ppermute | solution.py:10
  52.3 0.6 gather_fusion.4
  52.9 0.8 broadcast_select_fusion
  53.7 1.3 collective-permute-start.7
  55.4 1.3 fusion.25
  56.7 1.3 fusion.21
  58.0 1.0 copy.14
  59.0 1.0 copy.15
  60.0 1.3 fusion.17
  61.3 1.0 copy.16
  62.3 1.8 collective-permute-done.7
  64.4 1.0 copy.17
  65.8 0.7 copy-done.4
  68.5 1.0 multiply_convert_fusion
  69.5 0.8 gather_fusion.6
  71.0 0.9 multiply_bitcast_fusion.3
  71.9 1.5 collective-permute-start.8
  73.3 0.6 gather_fusion.5
  73.9 0.7 gather_fusion.8
  75.3 0.9 multiply_bitcast_fusion.1
  76.2 0.8 gather_fusion.9
  77.7 0.9 multiply_bitcast_fusion
  78.6 0.6 collective-permute-start.11
  79.1 0.7 gather_fusion.7
  81.3 2.4 %collective-permute-start.9 = (f32[8,128,128]{2,0,1:T(8,128)S(1)}, f32[8,128,128]{2,0,1:T(8,128)S(1)}, u32[]{:S(2)}, u32[]{:S(2)}) collective-permute-start(f32[8,128,128]{2,0,1:T(8,128)S(1)} %multiply_bitcast_fusion.2), channel_id=1, source_target_pairs={{4,0},{8,4},{12,8},{16,12},{20,16},{24,20},{28,24},{0,28},{5,1},{9... | collective-permute-start | bytes 1572872 | tf_op jit(solution)/shard_map/ppermute | solution.py:10
  84.1 9.4 %collective-permute-done.10 = f32[8,128,128]{2,0,1:T(8,128)} collective-permute-done((f32[8,128,128]{2,0,1:T(8,128)}, f32[8,128,128]{2,0,1:T(8,128)}, u32[]{:S(2)}, u32[]{:S(2)}) %collective-permute-start.10) | collective-permute-done | bytes 524320 | tf_op jit(solution)/shard_map/ppermute | solution.py:10
  93.4 1.4 fusion.65
  94.8 3.1 %collective-permute-done.11 = f32[8,128,128]{2,0,1:T(8,128)} collective-permute-done((f32[8,128,128]{2,0,1:T(8,128)}, f32[8,128,128]{2,0,1:T(8,128)}, u32[]{:S(2)}, u32[]{:S(2)}) %collective-permute-start.11) | collective-permute-done | bytes 524320 | tf_op jit(solution)/shard_map/ppermute | solution.py:10
  97.9 1.4 fusion.68
  99.4 1.4 convolution_add_fusion.1
  100.8 5.3 %collective-permute-done.9 = f32[8,128,128]{2,0,1:T(8,128)S(1)} collective-permute-done((f32[8,128,128]{2,0,1:T(8,128)S(1)}, f32[8,128,128]{2,0,1:T(8,128)S(1)}, u32[]{:S(2)}, u32[]{:S(2)}) %collective-permute-start.9) | collective-permute-done | bytes 524320 | tf_op jit(solution)/shard_map/ppermute | solution.py:10
  106.7 1.0 copy-done.2
  107.7 1.0 convolution_bitcast_fusion
  108.8 1.8 fusion.89
  110.6 52.1 %all-reduce.2.cloned.1.call-done = f32[512,128]{0,1:T(8,128)} async-done(((f32[512,128]{0,1:T(8,128)}), f32[512,128]{0,1:T(8,128)}) %all-reduce.2.cloned.1.call-update) | async-done | bytes 262160 | tf_op jit(solution)/shard_map/psum | solution.py:88
  162.7 1.8 copy.12
  164.5 43.6 %reduce-scatter.2.cloned.1.call-done = f32[1024,128]{1,0:T(8,128)} async-done(((f32[1024,512]{1,0:T(8,128)}), f32[1024,128]{1,0:T(8,128)}) %reduce-scatter.2.cloned.1.call-update) | async-done | bytes 524304 | tf_op jit(solution)/shard_map/reduce_scatter | solution.py:92
  208.1 1.8 convert_element_type.89
  (109 shorter events, 8.7 us)
Async XLA Ops:
  7.2 35.1 %copy-start = (bf16[512,128]{1,0:T(8,128)(2,1)S(1)}, bf16[512,128]{1,0:T(8,128)(2,1)}, u32[]{:S(2)}) copy-start(bf16[512,128]{1,0:T(8,128)(2,1)} %param.10) | copy-start | bytes 393220
  7.2 35.1 %all-gather.2.cloned.1.call-start = ((), (), s32[]{:S(2)}) async-start(), calls=%async_computation.1 | async-start | bytes 1310720 | tf_op jit(solution)/shard_map/all_gather | solution.py:28
  7.9 154.8 %all-reduce.2.cloned.1.call-start = ((), (), s32[]{:S(2)}) async-start(), calls=%async_computation.3 | async-start | bytes 524288 | tf_op jit(solution)/shard_map/psum | solution.py:88
  8.7 11.6 %collective-permute-start = (s32[8]{0:T(128)S(1)}, s32[8]{0:T(128)S(1)}, u32[]{:S(2)}, u32[]{:S(2)}) collective-permute-start(s32[8]{0:T(128)S(1)} %get-tuple-element.32), channel_id=1, source_target_pairs={{8,0},{12,4},{16,8},{20,12},{24,16},{28,20},{0,24},{4,28},{9,1},{1... | collective-permute-start | bytes 104 | tf_op jit(solution)/shard_map/ppermute | solution.py:10
  12.6 7.7 %collective-permute-start.2 = (s32[8]{0:T(128)S(1)}, s32[8]{0:T(128)S(1)}, u32[]{:S(2)}, u32[]{:S(2)}) collective-permute-start(s32[8]{0:T(128)S(1)} %get-tuple-element.31), channel_id=1, source_target_pairs={{4,0},{8,4},{12,8},{16,12},{20,16},{24,20},{28,24},{0,28},{5,1},{9... | collective-permute-start | bytes 104 | tf_op jit(solution)/shard_map/ppermute | solution.py:10
  12.6 7.7 %collective-permute-start.4 = (s32[8]{0:T(128)S(1)}, s32[8]{0:T(128)S(1)}, u32[]{:S(2)}, u32[]{:S(2)}) collective-permute-start(s32[8]{0:T(128)S(1)} %get-tuple-element.30), channel_id=1, source_target_pairs={{28,0},{0,4},{4,8},{8,12},{12,16},{16,20},{20,24},{24,28},{29,1},{... | collective-permute-start | bytes 104 | tf_op jit(solution)/shard_map/ppermute | solution.py:10
  13.1 7.8 %collective-permute-start.6 = (s32[8]{0:T(128)S(1)}, s32[8]{0:T(128)S(1)}, u32[]{:S(2)}, u32[]{:S(2)}) collective-permute-start(s32[8]{0:T(128)S(1)} %get-tuple-element.29), channel_id=1, source_target_pairs={{24,0},{28,4},{0,8},{4,12},{8,16},{12,20},{16,24},{20,28},{25,1},{... | collective-permute-start | bytes 104 | tf_op jit(solution)/shard_map/ppermute | solution.py:10
  20.2 25.7 %copy-start.19 = (s32[8]{0:T(128)}, s32[8]{0:T(128)S(1)}, u32[]{:S(2)}) copy-start(s32[8]{0:T(128)S(1)} %collective-permute-done) | copy-start | bytes 100
  20.3 25.7 %copy-start.27 = (s32[8]{0:T(128)}, s32[8]{0:T(128)S(1)}, u32[]{:S(2)}) copy-start(s32[8]{0:T(128)S(1)} %collective-permute-done.2) | copy-start | bytes 100
  20.3 25.7 %copy-start.23 = (s32[8]{0:T(128)}, s32[8]{0:T(128)S(1)}, u32[]{:S(2)}) copy-start(s32[8]{0:T(128)S(1)} %collective-permute-done.4) | copy-start | bytes 100
  20.9 25.0 %copy-start.21 = (s32[8]{0:T(128)}, s32[8]{0:T(128)S(1)}, u32[]{:S(2)}) copy-start(s32[8]{0:T(128)S(1)} %collective-permute-done.6) | copy-start | bytes 100
  22.6 23.4 %copy-start.1 = (bf16[1,5,8,128,128]{4,3,2,1,0:T(8,128)(2,1)S(1)}, bf16[1,5,8,128,128]{4,3,2,1,0:T(8,128)(2,1)}, u32[]{:S(2)}) copy-start(bf16[1,5,8,128,128]{4,3,2,1,0:T(8,128)(2,1)} %param.11) | copy-start | bytes 3932164
  44.6 10.8 %collective-permute-start.1 = (bf16[8,128,128]{2,1,0:T(8,128)(2,1)S(1)}, bf16[8,128,128]{2,1,0:T(8,128)(2,1)}, u32[]{:S(2)}, u32[]{:S(2)}) collective-permute-start(bf16[8,128,128]{2,1,0:T(8,128)(2,1)S(1)} %broadcast_select_fusion.3), channel_id=1, source_target_pairs={{24,0},{28,4},{0,8},{4,12},{8,16},{12,20},{16,24},{20,28},{25,1},{... | collective-permute-start | bytes 786440 | tf_op jit(solution)/shard_map/ppermute | solution.py:10
  46.7 2.2 %copy-start.26 = (pred[8]{0:T(512)(128)(4,1)S(1)}, pred[8]{0:T(512)(128)(4,1)}, u32[]{:S(2)}) copy-start(pred[8]{0:T(512)(128)(4,1)} %compare_and_fusion.6) | copy-start | bytes 28
  46.7 6.2 %copy-start.25 = (pred[8]{0:T(512)(128)(4,1)S(1)}, pred[8]{0:T(512)(128)(4,1)}, u32[]{:S(2)}) copy-start(pred[8]{0:T(512)(128)(4,1)} %compare_and_fusion.5) | copy-start | bytes 28
  48.0 8.6 %collective-permute-start.3 = (bf16[8,128,128]{2,1,0:T(8,128)(2,1)S(1)}, bf16[8,128,128]{2,1,0:T(8,128)(2,1)}, u32[]{:S(2)}, u32[]{:S(2)}) collective-permute-start(bf16[8,128,128]{2,1,0:T(8,128)(2,1)S(1)} %broadcast_select_fusion.2), channel_id=1, source_target_pairs={{28,0},{0,4},{4,8},{8,12},{12,16},{16,20},{20,24},{24,28},{29,1},{... | collective-permute-start | bytes 786440 | tf_op jit(solution)/shard_map/ppermute | solution.py:10
  49.6 10.4 %collective-permute-start.5 = (bf16[8,128,128]{2,1,0:T(8,128)(2,1)}, bf16[8,128,128]{2,1,0:T(8,128)(2,1)}, u32[]{:S(2)}, u32[]{:S(2)}) collective-permute-start(bf16[8,128,128]{2,1,0:T(8,128)(2,1)} %broadcast_select_fusion.1), channel_id=1, source_target_pairs={{4,0},{8,4},{12,8},{16,12},{20,16},{24,20},{28,24},{0,28},{5,1},{9... | collective-permute-start | bytes 786440 | tf_op jit(solution)/shard_map/ppermute | solution.py:10
  53.7 10.4 %collective-permute-start.7 = (bf16[8,128,128]{2,1,0:T(8,128)(2,1)}, bf16[8,128,128]{2,1,0:T(8,128)(2,1)S(1)}, u32[]{:S(2)}, u32[]{:S(2)}) collective-permute-start(bf16[8,128,128]{2,1,0:T(8,128)(2,1)} %broadcast_select_fusion), channel_id=1, source_target_pairs={{8,0},{12,4},{16,8},{20,12},{24,16},{28,20},{0,24},{4,28},{9,1},{1... | collective-permute-start | bytes 786440 | tf_op jit(solution)/shard_map/ppermute | solution.py:10
  62.3 3.1 %copy-start.3 = (f32[8,128,128]{1,0,2:T(8,128)S(1)}, f32[8,128,128]{1,0,2:T(8,128)}, u32[]{:S(2)}) copy-start(f32[8,128,128]{1,0,2:T(8,128)} %copy.14) | copy-start | bytes 1572868
  65.4 1.0 copy-start.4
  65.4 1.4 copy-start.5
  66.5 1.1 copy-start.6
  67.5 0.9 copy-start.7
  68.5 1.8 copy-start.17
  69.5 1.5 copy-start.12
  70.9 3.7 %copy-start.16 = (pred[8]{0:T(512)(128)(4,1)S(1)}, pred[8]{0:T(512)(128)(4,1)}, u32[]{:S(2)}) copy-start(pred[8]{0:T(512)(128)(4,1)} %get-tuple-element.27) | copy-start | bytes 28
  71.9 27.5 %collective-permute-start.8 = (f32[8,128,128]{2,0,1:T(8,128)}, f32[8,128,128]{2,0,1:T(8,128)}, u32[]{:S(2)}, u32[]{:S(2)}) collective-permute-start(f32[8,128,128]{2,0,1:T(8,128)} %multiply_bitcast_fusion.3), channel_id=1, source_target_pairs={{8,0},{12,4},{16,8},{20,12},{24,16},{28,20},{0,24},{4,28},{9,1},{1... | collective-permute-start | bytes 1572872 | tf_op jit(solution)/shard_map/ppermute | solution.py:10
  73.9 1.4 copy-start.11
  75.0 2.0 copy-start.15
  76.2 17.2 %collective-permute-start.10 = (f32[8,128,128]{2,0,1:T(8,128)}, f32[8,128,128]{2,0,1:T(8,128)}, u32[]{:S(2)}, u32[]{:S(2)}) collective-permute-start(f32[8,128,128]{2,0,1:T(8,128)} %multiply_bitcast_fusion.1), channel_id=1, source_target_pairs={{28,0},{0,4},{4,8},{8,12},{12,16},{16,20},{20,24},{24,28},{29,1},{... | collective-permute-start | bytes 1572872 | tf_op jit(solution)/shard_map/ppermute | solution.py:10
  76.2 1.5 copy-start.10
  77.4 2.5 %copy-start.14 = (pred[8]{0:T(512)(128)(4,1)S(1)}, pred[8]{0:T(512)(128)(4,1)}, u32[]{:S(2)}) copy-start(pred[8]{0:T(512)(128)(4,1)} %get-tuple-element.23) | copy-start | bytes 28
  77.7 2.6 %copy-start.13 = (pred[8]{0:T(512)(128)(4,1)S(1)}, pred[8]{0:T(512)(128)(4,1)}, u32[]{:S(2)}) copy-start(pred[8]{0:T(512)(128)(4,1)} %get-tuple-element.7) | copy-start | bytes 28
  78.6 19.4 %collective-permute-start.11 = (f32[8,128,128]{2,0,1:T(8,128)}, f32[8,128,128]{2,0,1:T(8,128)}, u32[]{:S(2)}, u32[]{:S(2)}) collective-permute-start(f32[8,128,128]{2,0,1:T(8,128)} %multiply_bitcast_fusion), channel_id=1, source_target_pairs={{24,0},{28,4},{0,8},{4,12},{8,16},{12,20},{16,24},{20,28},{25,1},{... | collective-permute-start | bytes 1572872 | tf_op jit(solution)/shard_map/ppermute | solution.py:10
  80.2 0.7 copy-start.9
  80.8 2.8 %copy-start.8 = (pred[1,8]{1,0:T(4,128)(4,1)S(1)}, pred[1,8]{1,0:T(4,128)(4,1)}, u32[]{:S(2)}) copy-start(pred[1,8]{1,0:T(4,128)(4,1)} %get-tuple-element.34) | copy-start | bytes 28
  80.8 2.8 %copy-start.18 = (s32[1,8]{1,0:T(1,128)S(1)}, s32[1,8]{1,0:T(1,128)}, u32[]{:S(2)}) copy-start(s32[1,8]{1,0:T(1,128)} %slice.130) | copy-start | bytes 100
  81.0 12.4 %copy-start.24 = (s32[8]{0:T(128)S(1)}, s32[8]{0:T(128)}, u32[]{:S(2)}) copy-start(s32[8]{0:T(128)} %copy-done.23) | copy-start | bytes 100
  81.3 16.7 %copy-start.22 = (s32[8]{0:T(128)S(1)}, s32[8]{0:T(128)}, u32[]{:S(2)}) copy-start(s32[8]{0:T(128)} %copy-done.21) | copy-start | bytes 100
  81.3 24.8 %collective-permute-start.9 = (f32[8,128,128]{2,0,1:T(8,128)S(1)}, f32[8,128,128]{2,0,1:T(8,128)S(1)}, u32[]{:S(2)}, u32[]{:S(2)}) collective-permute-start(f32[8,128,128]{2,0,1:T(8,128)S(1)} %multiply_bitcast_fusion.2), channel_id=1, source_target_pairs={{4,0},{8,4},{12,8},{16,12},{20,16},{24,20},{28,24},{0,28},{5,1},{9... | collective-permute-start | bytes 1572872 | tf_op jit(solution)/shard_map/ppermute | solution.py:10
  84.1 15.3 %copy-start.20 = (s32[8]{0:T(128)S(1)}, s32[8]{0:T(128)}, u32[]{:S(2)}) copy-start(s32[8]{0:T(128)} %copy-done.19) | copy-start | bytes 100
  94.8 11.2 %copy-start.28 = (s32[8]{0:T(128)S(1)}, s32[8]{0:T(128)}, u32[]{:S(2)}) copy-start(s32[8]{0:T(128)} %copy-done.27) | copy-start | bytes 100
  106.5 1.2 copy-start.2
  108.8 99.3 %reduce-scatter.2.cloned.1.call-start = ((), (), s32[]{:S(2)}) async-start(), calls=%async_computation.2 | async-start | bytes 2621440 | tf_op jit(solution)/shard_map/reduce_scatter | solution.py:92
Sparse Core Ops, SparseCore 0:
  9.5 32.6 all-gather.1
  108.9 53.7 all-reduce.1
  165.0 43.0 reduce-scatter.1
where the time goes:
time: 217 us; the launch traced here: 216 us
  waiting for transfers between devices  136 us (63%)
  local copies, waits for them, and re-layouts  19.5 us (9%)
  matrix products  17.6 us (8%)
  other arithmetic  14.8 us (7%)
  starting transfers between devices  14.4 us (7%)
  between operations  14.4 us (7%)
    psum x1, waiting for transfers between devices, on_device(): grad_w = lax.psum(weight_term, 'blk')  52.1 us
    reduce_scatter x1, waiting for transfers between devices, on_device(): lax.psum_scatter(partial_grad, 'feat', scatter_dimension=1, tiled=True)  43.6 us
    all_gather x1, waiting for transfers between devices, on_device(): full_feats = lax.all_gather(node_feats, 'feat', axis=1, tiled=True)  19.6 us
    ppermute x12, waiting for transfers between devices, shifted(): return lax.ppermute(block, axis, route)  19.6 us
    ppermute x12, starting transfers between devices, shifted(): return lax.ppermute(block, axis, route)  14.3 us
    unnamed x61, local copies, waits for them, and re-layouts  5.8 us
    dot_general x4, matrix products, on_device(): jnp.einsum('cs,sif->cif', target_onehot, received, precision=lax.Precisio...  4.6 us
  transfers between devices with their start and end apart: 15, of which 7 were waited for; matrix products, arithmetic and copies ran while one was open for 17% of the time, Pallas kernels for 0%

commit v1 on v0

--- a/solution.py
+++ b/solution.py
@@ -2,6 +2,24 @@
 import jax.numpy as jnp
 from jax import lax
 from jax.sharding import PartitionSpec as P
+
+
+def laid_out(tiles, dim):
+    shape = list(tiles.shape[1:])
+    shape[dim] *= tiles.shape[0]
+    return jnp.moveaxis(tiles, 0, dim).reshape(shape)
+
+
+def collected_by_bits(x, axis):
+    count = lax.axis_size(axis)
+    tiles = x[None]
+    for level in range(count.bit_length() - 1):
+        bit = 1 << level
+        partner_block = lax.ppermute(tiles, axis, [(i, i ^ bit) for i in range(count)])
+        both = jnp.stack([tiles, partner_block])
+        upper = lax.axis_index(axis) >> level & 1
+        tiles = jnp.where(upper == 0, both, both[::-1]).reshape(-1, *x.shape)
+    return tiles
 
 
 def shifted(block, axis, distance):
@@ -25,7 +43,7 @@
     col_onehot = (
         (tile_col[0][:, None, :] == block_ids[None, :, None]) & live_slots[:, None, :]
     ).astype(jnp.float32)
-    full_feats = lax.all_gather(node_feats, "feat", axis=1, tiled=True)
+    full_feats = laid_out(collected_by_bits(node_feats, "feat"), 1)
     hidden = jnp.dot(full_feats, weight, preferred_element_type=jnp.float32).astype(jnp.bfloat16)
     panel_own = hidden.reshape(blocks, tile_side, feat_width)
     wanted_lists = {}

time: 217 us -> 194 us (0.89)
  waiting for transfers between devices: 136 us -> 84.8 us
  local copies, waits for them, and re-layouts: 19.5 us -> 26.9 us
  other arithmetic: 14.8 us -> 22 us
  matrix products: 17.6 us -> 24.5 us
  starting transfers between devices: 14.4 us -> 18.6 us
    psum x1, waiting for transfers between devices: 52.1 us -> 11.9 us  [on_device(): grad_w = lax.psum(weight_term, 'blk')]
    ppermute x0 -> x2, waiting for transfers between devices: none -> 22.5 us  [collected_by_bits(): lax.ppermute(tiles, axis, [(i, i ^ bit) for i in range(count)])]
    all_gather x1 -> x0, waiting for transfers between devices: 19.6 us -> none  [on_device(): full_feats = lax.all_gather(node_feats, 'feat', axis=1, tiled=True)]
    ppermute x12, waiting for transfers between devices: 19.6 us -> 7.09 us  [shifted(): return lax.ppermute(block, axis, route)]
    ppermute x0 -> x2, starting transfers between devices: none -> 5.77 us  [collected_by_bits(): lax.ppermute(tiles, axis, [(i, i ^ bit) for i in range(count)])]
    dot_general x5, matrix products: 1.74 us -> 5.41 us  [slot_products(): jnp.einsum('sji,sjf->sif', tile_value[0, offset], picked, preferred_eleme...]
    dot_general x5, local copies, waits for them, and re-layouts: 1.16 us -> 4.52 us  [slot_products(): jnp.einsum('sji,sjf->sif', tile_value[0, offset], picked, preferred_eleme...]
    mul x4, other arithmetic: 2.8 us -> 5.95 us  [on_device(): slot_products(offset)]
  transfers between devices with their start and end apart: 15 -> 16, of which waited for: 7 -> 5; matrix products, arithmetic and copies ran while one was open for 17% -> 28% of each run, Pallas kernels for 0% -> 0%
where the time goes in v1:
time: 194 us; the launch traced here: 193 us
  waiting for transfers between devices  84.8 us (44%)
  local copies, waits for them, and re-layouts  26.9 us (14%)
  matrix products  24.5 us (13%)
  other arithmetic  22 us (11%)
  starting transfers between devices  18.6 us (10%)
  between operations  16.1 us (8%)
    reduce_scatter x1, waiting for transfers between devices, on_device(): lax.psum_scatter(partial_grad, 'feat', scatter_dimension=1, tiled=True)  43.2 us
    ppermute x2, waiting for transfers between devices, collected_by_bits(): lax.ppermute(tiles, axis, [(i, i ^ bit) for i in range(count)])  22.5 us
    ppermute x12, starting transfers between devices, shifted(): return lax.ppermute(block, axis, route)  12.8 us
    psum x1, waiting for transfers between devices, on_device(): grad_w = lax.psum(weight_term, 'blk')  11.9 us
    ppermute x12, waiting for transfers between devices, shifted(): return lax.ppermute(block, axis, route)  7.09 us
    dot_general x4, local copies, waits for them, and re-layouts, on_device(): jnp.einsum('sij,sjf->sif', tile_value[0, offset], arrived, preferred_elem...  6.15 us
    mul x4, other arithmetic, on_device(): slot_products(offset)  5.95 us
    gather x5, local copies, waits for them, and re-layouts, slot_products(): picked = jnp.take(grad_blocks, tile_row[0, offset], axis=0)  5.78 us
  transfers between devices with their start and end apart: 16, of which 5 were waited for; matrix products, arithmetic and copies ran while one was open for 28% of the time, Pallas kernels for 0%

profile of v1, /device:TPU:0, one launch (start us, length us, event | category | flops | bytes accessed | tf_op | source)
XLA Modules:
  0.0 192.8 jit_solution(5395370869966958696)
XLA Ops:
  8.1 3.1 %collective-permute-start = (bf16[1,1024,128]{2,1,0:T(8,128)(2,1)}, bf16[1,1024,128]{2,1,0:T(8,128)(2,1)S(1)}, u32[]{:S(2)}, u32[]{:S(2)}) collective-permute-start(bf16[1,1024,128]{2,1,0:T(8,128)(2,1)} %bitcast.180), channel_id=1, source_target_pairs={{0,1},{1,0},{2,3},{3,2},{4,5},{5,4},{6,7},{7,6},{8,9},{9,8},{10,11... | collective-permute-start | bytes 786440 | tf_op jit(solution)/shard_map/ppermute | solution.py:18
  11.2 0.7 slice_bitcast_fusion.10
  11.9 2.4 %collective-permute-start.2 = (s32[8]{0:T(128)S(1)}, s32[8]{0:T(128)S(1)}, u32[]{:S(2)}, u32[]{:S(2)}) collective-permute-start(s32[8]{0:T(128)S(1)} %get-tuple-element.31), channel_id=1, source_target_pairs={{8,0},{12,4},{16,8},{20,12},{24,16},{28,20},{0,24},{4,28},{9,1},{1... | collective-permute-start | bytes 104 | tf_op jit(solution)/shard_map/ppermute | solution.py:28
  15.2 0.7 compare_and_fusion.9
  15.9 0.7 copy.30
  16.6 1.3 compare_and_fusion.2
  17.9 0.7 copy.29
  18.6 0.7 iota_compare_fusion.6
  19.3 0.6 fusion.82
  20.5 0.6 pad_clamp_fusion.2
  22.4 0.6 pad_clamp_fusion.6
  23.0 1.0 pad_maximum_fusion.1
  24.2 2.7 %collective-permute-start.1 = (bf16[2,1024,128]{2,1,0:T(8,128)(2,1)S(1)}, bf16[2,1024,128]{2,1,0:T(8,128)(2,1)S(1)}, u32[]{:S(2)}, u32[]{:S(2)}) collective-permute-start(bf16[2,1024,128]{2,1,0:T(8,128)(2,1)S(1)} %get-tuple-element.19), channel_id=1, source_target_pairs={{0,2},{1,3},{2,0},{3,1},{4,6},{5,7},{6,4},{7,5},{8,10},{9,11},{10,... | collective-permute-start | bytes 1572872 | tf_op jit(solution)/shard_map/ppermute | solution.py:18
  28.5 22.5 %collective-permute-done.1 = bf16[2,1024,128]{2,1,0:T(8,128)(2,1)S(1)} collective-permute-done((bf16[2,1024,128]{2,1,0:T(8,128)(2,1)S(1)}, bf16[2,1024,128]{2,1,0:T(8,128)(2,1)S(1)}, u32[]{:S(2)}, u32[]{:S(2)}) %collective-permute-start.1) | collective-permute-done | bytes 524320 | tf_op jit(solution)/shard_map/ppermute | solution.py:18
  52.4 0.6 gather_fusion.1
  53.0 0.8 broadcast_select_fusion.3
  53.8 0.9 collective-permute-start.3
  55.3 1.2 fusion.31
  56.5 1.3 copy.15
  58.4 1.4 broadcast_select_fusion.2
  59.8 0.7 gather_fusion.3
  60.6 1.4 broadcast_select_fusion.1
  62.0 2.6 %collective-permute-start.7 = (bf16[8,128,128]{2,1,0:T(8,128)(2,1)}, bf16[8,128,128]{2,1,0:T(8,128)(2,1)}, u32[]{:S(2)}, u32[]{:S(2)}) collective-permute-start(bf16[8,128,128]{2,1,0:T(8,128)(2,1)} %broadcast_select_fusion.1), channel_id=1, source_target_pairs={{4,0},{8,4},{12,8},{16,12},{20,16},{24,20},{28,24},{0,28},{5,1},{9... | collective-permute-start | bytes 786440 | tf_op jit(solution)/shard_map/ppermute | solution.py:28
  64.6 0.7 gather_fusion.4
  65.3 0.8 broadcast_select_fusion
  66.1 1.1 collective-permute-start.9
  67.3 1.2 fusion.9
  68.4 1.3 fusion.27
  69.7 2.1 %fusion.23 = f32[8,128,128]{2,1,0:T(8,128)} fusion(bf16[8,128,128]{2,1,0:T(8,128)(2,1)} %collective-permute-done.5, bf16[1,5,8,128,128]{4,3,2,1,0:T(8,128)(2,1)S(1)} %copy-done.1), kind=kOutput, calls=%fused_computation.53 | convolution fusion | flops 33554432 | bytes 1048576 | tf_op jit(solution)/shard_map/sij,sjf->sif/dot_general | solution.py:64
  71.8 1.0 copy.16
  72.8 2.1 %copy.17 = f32[8,128,128]{1,0,2:T(8,128)} copy(f32[8,128,128]{2,1,0:T(8,128)} %fusion.23) | data formatting | bytes 1048576 | tf_op jit(solution)/shard_map/sij,sjf->sif/dot_general | solution.py:64
  74.9 1.3 fusion.19
  76.2 1.0 copy.18
  77.2 1.1 fusion.15
  78.3 2.0 %copy.19 = f32[8,128,128]{1,0,2:T(8,128)} copy(f32[8,128,128]{2,1,0:T(8,128)} %fusion.15) | data formatting | bytes 1048576 | tf_op jit(solution)/shard_map/sij,sjf->sif/dot_general | solution.py:64
  80.4 1.5 convolution_add_fusion.5
  83.9 1.0 multiply_convert_fusion
  84.8 0.8 gather_fusion.6
  86.1 1.0 copy.21
  87.1 1.9 %multiply_bitcast_fusion.3 = f32[8,128,128]{2,0,1:T(8,128)} fusion(f32[8,128,128]{1,0,2:T(8,128)} %copy.21, f32[8]{0:T(128)S(1)} %copy-done.11), kind=kLoop, calls=%fused_computation.37 | loop fusion | flops 131072 | bytes 1048608 | tf_op jit(solution)/shard_map/mul | solution.py:92
  89.0 1.9 collective-permute-start.10
  91.5 1.4 gather_fusion.8
  92.9 1.3 fusion.17
  94.2 1.0 copy.23
  95.2 1.9 %multiply_bitcast_fusion.1 = f32[8,128,128]{2,0,1:T(8,128)} fusion(f32[8,128,128]{1,0,2:T(8,128)} %copy.23, f32[8]{0:T(128)S(1)} %copy-done.10), kind=kLoop, calls=%fused_computation.35 | loop fusion | flops 131072 | bytes 1048608 | tf_op jit(solution)/shard_map/mul | solution.py:92
  97.2 1.5 gather_fusion.9
  98.7 1.3 fusion.13
  100.0 1.0 copy.24
  101.0 2.0 %multiply_bitcast_fusion = f32[8,128,128]{2,0,1:T(8,128)} fusion(f32[8,128,128]{1,0,2:T(8,128)} %copy.24, f32[8]{0:T(128)S(1)} %copy-done.9), kind=kLoop, calls=%fused_computation.34 | loop fusion | flops 131072 | bytes 1048608 | tf_op jit(solution)/shard_map/mul | solution.py:92
  103.2 1.4 gather_fusion.7
  104.9 2.1 %fusion.21 = f32[8,128,128]{2,1,0:T(8,128)} fusion(bf16[8,128,128]{2,1,0:T(8,128)(2,1)} %gather_fusion.7, pred[8]{0:T(512)(128)(4,1)S(1)} %copy-done.12, bf16[1,5,8,128,128]{4,3,2,1,0:T(8,128)(2,1)S(1)} %copy-done.1), kind=kOutput, calls=%fused_computation.51 | convolution fusion | flops 33685504 | bytes 1049088 | tf_op jit(solution)/shard_map/sji,sjf->sif/dot_general | solution.py:79
  107.0 1.3 copy.22
  108.7 2.7 %collective-permute-start.11 = (f32[8,128,128]{2,0,1:T(8,128)S(1)}, f32[8,128,128]{2,0,1:T(8,128)S(1)}, u32[]{:S(2)}, u32[]{:S(2)}) collective-permute-start(f32[8,128,128]{2,0,1:T(8,128)S(1)} %multiply_bitcast_fusion.2), channel_id=1, source_target_pairs={{4,0},{8,4},{12,8},{16,12},{20,16},{24,20},{28,24},{0,28},{5,1},{9... | collective-permute-start | bytes 1572872 | tf_op jit(solution)/shard_map/ppermute | solution.py:28
  111.8 1.4 fusion.67
  113.3 5.7 %collective-permute-done.13 = f32[8,128,128]{2,0,1:T(8,128)} collective-permute-done((f32[8,128,128]{2,0,1:T(8,128)}, f32[8,128,128]{2,0,1:T(8,128)}, u32[]{:S(2)}, u32[]{:S(2)}) %collective-permute-start.13) | collective-permute-done | bytes 524320 | tf_op jit(solution)/shard_map/ppermute | solution.py:28
  119.0 1.4 fusion.70
  120.4 1.4 convolution_add_fusion.1
  121.8 1.3 collective-permute-done.11
  123.7 1.8 fusion.91
  125.6 1.1 fusion.92
  126.8 43.2 %reduce-scatter.2.cloned.1.call-done = f32[1024,128]{1,0:T(8,128)} async-done(((f32[1024,512]{1,0:T(8,128)}), f32[1024,128]{1,0:T(8,128)}) %reduce-scatter.2.cloned.1.call-update) | async-done | bytes 524304 | tf_op jit(solution)/shard_map/reduce_scatter | solution.py:110
  169.9 1.8 convert_element_type.89
  171.7 11.9 %all-reduce.2.cloned.1.call-done = f32[512,128]{1,0:T(8,128)} async-done(((f32[512,128]{1,0:T(8,128)}), f32[512,128]{1,0:T(8,128)}) %all-reduce.2.cloned.1.call-update) | async-done | bytes 262160 | tf_op jit(solution)/shard_map/psum | solution.py:106
  183.6 1.7 copy.32
  (111 shorter events, 11.9 us)
Async XLA Ops:
  8.0 43.8 %copy-start = (bf16[512,128]{1,0:T(8,128)(2,1)S(1)}, bf16[512,128]{1,0:T(8,128)(2,1)}, u32[]{:S(2)}) copy-start(bf16[512,128]{1,0:T(8,128)(2,1)} %param.10) | copy-start | bytes 393220
  8.0 161.9 %reduce-scatter.2.cloned.1.call-start = ((), (), s32[]{:S(2)}) async-start(), calls=%async_computation.1 | async-start | bytes 2621440 | tf_op jit(solution)/shard_map/reduce_scatter | solution.py:110
  8.1 14.9 %collective-permute-start = (bf16[1,1024,128]{2,1,0:T(8,128)(2,1)}, bf16[1,1024,128]{2,1,0:T(8,128)(2,1)S(1)}, u32[]{:S(2)}, u32[]{:S(2)}) collective-permute-start(bf16[1,1024,128]{2,1,0:T(8,128)(2,1)} %bitcast.180), channel_id=1, source_target_pairs={{0,1},{1,0},{2,3},{3,2},{4,5},{5,4},{6,7},{7,6},{8,9},{9,8},{10,11... | collective-permute-start | bytes 786440 | tf_op jit(solution)/shard_map/ppermute | solution.py:18
  11.9 9.9 %collective-permute-start.2 = (s32[8]{0:T(128)S(1)}, s32[8]{0:T(128)S(1)}, u32[]{:S(2)}, u32[]{:S(2)}) collective-permute-start(s32[8]{0:T(128)S(1)} %get-tuple-element.31), channel_id=1, source_target_pairs={{8,0},{12,4},{16,8},{20,12},{24,16},{28,20},{0,24},{4,28},{9,1},{1... | collective-permute-start | bytes 104 | tf_op jit(solution)/shard_map/ppermute | solution.py:28
  14.3 7.4 %collective-permute-start.4 = (s32[8]{0:T(128)S(1)}, s32[8]{0:T(128)S(1)}, u32[]{:S(2)}, u32[]{:S(2)}) collective-permute-start(s32[8]{0:T(128)S(1)} %get-tuple-element.30), channel_id=1, source_target_pairs={{4,0},{8,4},{12,8},{16,12},{20,16},{24,20},{28,24},{0,28},{5,1},{9... | collective-permute-start | bytes 104 | tf_op jit(solution)/shard_map/ppermute | solution.py:28
  14.3 8.0 %collective-permute-start.6 = (s32[8]{0:T(128)S(1)}, s32[8]{0:T(128)S(1)}, u32[]{:S(2)}, u32[]{:S(2)}) collective-permute-start(s32[8]{0:T(128)S(1)} %get-tuple-element.29), channel_id=1, source_target_pairs={{28,0},{0,4},{4,8},{8,12},{12,16},{16,20},{20,24},{24,28},{29,1},{... | collective-permute-start | bytes 104 | tf_op jit(solution)/shard_map/ppermute | solution.py:28
  14.8 8.1 %collective-permute-start.8 = (s32[8]{0:T(128)S(1)}, s32[8]{0:T(128)S(1)}, u32[]{:S(2)}, u32[]{:S(2)}) collective-permute-start(s32[8]{0:T(128)S(1)} %get-tuple-element.28), channel_id=1, source_target_pairs={{24,0},{28,4},{0,8},{4,12},{8,16},{12,20},{16,24},{20,28},{25,1},{... | collective-permute-start | bytes 104 | tf_op jit(solution)/shard_map/ppermute | solution.py:28
  21.7 1.3 copy-start.18
  21.8 1.2 copy-start.25
  22.4 5.1 %copy-start.22 = (s32[8]{0:T(128)}, s32[8]{0:T(128)S(1)}, u32[]{:S(2)}) copy-start(s32[8]{0:T(128)S(1)} %collective-permute-done.6) | copy-start | bytes 100
  23.0 5.0 %copy-start.20 = (s32[8]{0:T(128)}, s32[8]{0:T(128)S(1)}, u32[]{:S(2)}) copy-start(s32[8]{0:T(128)S(1)} %collective-permute-done.8) | copy-start | bytes 100
  24.2 26.8 %collective-permute-start.1 = (bf16[2,1024,128]{2,1,0:T(8,128)(2,1)S(1)}, bf16[2,1024,128]{2,1,0:T(8,128)(2,1)S(1)}, u32[]{:S(2)}, u32[]{:S(2)}) collective-permute-start(bf16[2,1024,128]{2,1,0:T(8,128)(2,1)S(1)} %get-tuple-element.19), channel_id=1, source_target_pairs={{0,2},{1,3},{2,0},{3,1},{4,6},{5,7},{6,4},{7,5},{8,10},{9,11},{10,... | collective-permute-start | bytes 1572872 | tf_op jit(solution)/shard_map/ppermute | solution.py:18
  51.9 3.4 %copy-start.1 = (bf16[1,5,8,128,128]{4,3,2,1,0:T(8,128)(2,1)S(1)}, bf16[1,5,8,128,128]{4,3,2,1,0:T(8,128)(2,1)}, u32[]{:S(2)}) copy-start(bf16[1,5,8,128,128]{4,3,2,1,0:T(8,128)(2,1)} %param.11) | copy-start | bytes 3932164
  53.8 14.7 %collective-permute-start.3 = (bf16[8,128,128]{2,1,0:T(8,128)(2,1)}, bf16[8,128,128]{2,1,0:T(8,128)(2,1)}, u32[]{:S(2)}, u32[]{:S(2)}) collective-permute-start(bf16[8,128,128]{2,1,0:T(8,128)(2,1)} %broadcast_select_fusion.3), channel_id=1, source_target_pairs={{24,0},{28,4},{0,8},{4,12},{8,16},{12,20},{16,24},{20,28},{25,1},{... | collective-permute-start | bytes 786440 | tf_op jit(solution)/shard_map/ppermute | solution.py:28
  58.4 6.9 %copy-start.24 = (pred[8]{0:T(512)(128)(4,1)S(1)}, pred[8]{0:T(512)(128)(4,1)}, u32[]{:S(2)}) copy-start(pred[8]{0:T(512)(128)(4,1)} %compare_and_fusion.5) | copy-start | bytes 28
  59.8 9.9 %collective-permute-start.5 = (bf16[8,128,128]{2,1,0:T(8,128)(2,1)}, bf16[8,128,128]{2,1,0:T(8,128)(2,1)}, u32[]{:S(2)}, u32[]{:S(2)}) collective-permute-start(bf16[8,128,128]{2,1,0:T(8,128)(2,1)} %broadcast_select_fusion.2), channel_id=1, source_target_pairs={{28,0},{0,4},{4,8},{8,12},{12,16},{16,20},{20,24},{24,28},{29,1},{... | collective-permute-start | bytes 786440 | tf_op jit(solution)/shard_map/ppermute | solution.py:28
  62.0 12.9 %collective-permute-start.7 = (bf16[8,128,128]{2,1,0:T(8,128)(2,1)}, bf16[8,128,128]{2,1,0:T(8,128)(2,1)}, u32[]{:S(2)}, u32[]{:S(2)}) collective-permute-start(bf16[8,128,128]{2,1,0:T(8,128)(2,1)} %broadcast_select_fusion.1), channel_id=1, source_target_pairs={{4,0},{8,4},{12,8},{16,12},{20,16},{24,20},{28,24},{0,28},{5,1},{9... | collective-permute-start | bytes 786440 | tf_op jit(solution)/shard_map/ppermute | solution.py:28
  66.1 11.1 %collective-permute-start.9 = (bf16[8,128,128]{2,1,0:T(8,128)(2,1)}, bf16[8,128,128]{2,1,0:T(8,128)(2,1)S(1)}, u32[]{:S(2)}, u32[]{:S(2)}) collective-permute-start(bf16[8,128,128]{2,1,0:T(8,128)(2,1)} %broadcast_select_fusion), channel_id=1, source_target_pairs={{8,0},{12,4},{16,8},{20,12},{24,16},{28,20},{0,24},{4,28},{9,1},{1... | collective-permute-start | bytes 786440 | tf_op jit(solution)/shard_map/ppermute | solution.py:28
  77.2 3.2 %copy-start.2 = (f32[8,128,128]{2,0,1:T(8,128)S(1)}, f32[8,128,128]{2,0,1:T(8,128)}, u32[]{:S(2)}) copy-start(f32[8,128,128]{2,0,1:T(8,128)} %fusion.9) | copy-start | bytes 1572868
  80.4 1.5 copy-start.3
  80.4 1.9 copy-start.4
  81.9 1.0 copy-start.5
  82.9 0.9 copy-start.6
  83.9 1.8 copy-start.16
  84.8 2.2 %copy-start.11 = (f32[8]{0:T(128)S(1)}, f32[8]{0:T(128)}, u32[]{:S(2)}) copy-start(f32[8]{0:T(128)} %get-tuple-element.36) | copy-start | bytes 100
  87.1 5.8 %copy-start.15 = (pred[8]{0:T(512)(128)(4,1)S(1)}, pred[8]{0:T(512)(128)(4,1)}, u32[]{:S(2)}) copy-start(pred[8]{0:T(512)(128)(4,1)} %get-tuple-element.26) | copy-start | bytes 28
  89.0 31.4 %collective-permute-start.10 = (f32[8,128,128]{2,0,1:T(8,128)}, f32[8,128,128]{2,0,1:T(8,128)}, u32[]{:S(2)}, u32[]{:S(2)}) collective-permute-start(f32[8,128,128]{2,0,1:T(8,128)} %multiply_bitcast_fusion.3), channel_id=1, source_target_pairs={{8,0},{12,4},{16,8},{20,12},{24,16},{28,20},{0,24},{4,28},{9,1},{1... | collective-permute-start | bytes 1572872 | tf_op jit(solution)/shard_map/ppermute | solution.py:28
  91.5 3.7 %copy-start.10 = (f32[8]{0:T(128)S(1)}, f32[8]{0:T(128)}, u32[]{:S(2)}) copy-start(f32[8]{0:T(128)} %get-tuple-element.35) | copy-start | bytes 100
  94.2 4.5 %copy-start.14 = (pred[8]{0:T(512)(128)(4,1)S(1)}, pred[8]{0:T(512)(128)(4,1)}, u32[]{:S(2)}) copy-start(pred[8]{0:T(512)(128)(4,1)} %get-tuple-element.24) | copy-start | bytes 28
  97.1 14.7 %collective-permute-start.12 = (f32[8,128,128]{2,0,1:T(8,128)}, f32[8,128,128]{2,0,1:T(8,128)}, u32[]{:S(2)}, u32[]{:S(2)}) collective-permute-start(f32[8,128,128]{2,0,1:T(8,128)} %multiply_bitcast_fusion.1), channel_id=1, source_target_pairs={{28,0},{0,4},{4,8},{8,12},{12,16},{16,20},{20,24},{24,28},{29,1},{... | collective-permute-start | bytes 1572872 | tf_op jit(solution)/shard_map/ppermute | solution.py:28
  97.2 3.9 %copy-start.9 = (f32[8]{0:T(128)S(1)}, f32[8]{0:T(128)}, u32[]{:S(2)}) copy-start(f32[8]{0:T(128)} %get-tuple-element.34) | copy-start | bytes 100
  100.0 4.6 %copy-start.13 = (pred[8]{0:T(512)(128)(4,1)S(1)}, pred[8]{0:T(512)(128)(4,1)}, u32[]{:S(2)}) copy-start(pred[8]{0:T(512)(128)(4,1)} %get-tuple-element.22) | copy-start | bytes 28
  101.0 3.9 %copy-start.12 = (pred[8]{0:T(512)(128)(4,1)S(1)}, pred[8]{0:T(512)(128)(4,1)}, u32[]{:S(2)}) copy-start(pred[8]{0:T(512)(128)(4,1)} %get-tuple-element.4) | copy-start | bytes 28
  103.0 16.0 %collective-permute-start.13 = (f32[8,128,128]{2,0,1:T(8,128)}, f32[8,128,128]{2,0,1:T(8,128)}, u32[]{:S(2)}, u32[]{:S(2)}) collective-permute-start(f32[8,128,128]{2,0,1:T(8,128)} %multiply_bitcast_fusion), channel_id=1, source_target_pairs={{24,0},{28,4},{0,8},{4,12},{8,16},{12,20},{16,24},{20,28},{25,1},{... | collective-permute-start | bytes 1572872 | tf_op jit(solution)/shard_map/ppermute | solution.py:28
  104.9 3.4 %copy-start.8 = (f32[8]{0:T(128)S(1)}, f32[8]{0:T(128)}, u32[]{:S(2)}) copy-start(f32[8]{0:T(128)} %get-tuple-element.32) | copy-start | bytes 100
  108.3 3.1 %copy-start.7 = (pred[1,8]{1,0:T(4,128)(4,1)S(1)}, pred[1,8]{1,0:T(4,128)(4,1)}, u32[]{:S(2)}) copy-start(pred[1,8]{1,0:T(4,128)(4,1)} %get-tuple-element.33) | copy-start | bytes 28
  108.3 3.1 %copy-start.17 = (s32[1,8]{1,0:T(1,128)S(1)}, s32[1,8]{1,0:T(1,128)}, u32[]{:S(2)}) copy-start(s32[1,8]{1,0:T(1,128)} %slice.130) | copy-start | bytes 100
  108.5 3.4 %copy-start.23 = (s32[8]{0:T(128)S(1)}, s32[8]{0:T(128)}, u32[]{:S(2)}) copy-start(s32[8]{0:T(128)} %copy-done.22) | copy-start | bytes 100
  108.7 10.3 %copy-start.21 = (s32[8]{0:T(128)S(1)}, s32[8]{0:T(128)}, u32[]{:S(2)}) copy-start(s32[8]{0:T(128)} %copy-done.20) | copy-start | bytes 100
  108.7 14.4 %collective-permute-start.11 = (f32[8,128,128]{2,0,1:T(8,128)S(1)}, f32[8,128,128]{2,0,1:T(8,128)S(1)}, u32[]{:S(2)}, u32[]{:S(2)}) collective-permute-start(f32[8,128,128]{2,0,1:T(8,128)S(1)} %multiply_bitcast_fusion.2), channel_id=1, source_target_pairs={{4,0},{8,4},{12,8},{16,12},{20,16},{24,20},{28,24},{0,28},{5,1},{9... | collective-permute-start | bytes 1572872 | tf_op jit(solution)/shard_map/ppermute | solution.py:28
  111.8 8.6 %copy-start.19 = (s32[8]{0:T(128)S(1)}, s32[8]{0:T(128)}, u32[]{:S(2)}) copy-start(s32[8]{0:T(128)} %copy-done.18) | copy-start | bytes 100
  113.2 9.9 %copy-start.26 = (s32[8]{0:T(128)S(1)}, s32[8]{0:T(128)}, u32[]{:S(2)}) copy-start(s32[8]{0:T(128)} %copy-done.25) | copy-start | bytes 100
  125.5 58.1 %all-reduce.2.cloned.1.call-start = ((), (), s32[]{:S(2)}) async-start(), calls=%async_computation.2 | async-start | bytes 524288 | tf_op jit(solution)/shard_map/psum | solution.py:106
Sparse Core Ops, SparseCore 0:
  125.7 44.2 reduce-scatter.1
Sparse Core Ops, SparseCore 1:
  129.6 54.0 all-reduce.1
